TPU v7x, 32 devices: a whole 2x2x4 slice. The times are simulated.
32 devices in a mesh: row: 8 (over y, x, core), col: 4 (over z).
Axes of the slice: x: 2, y: 2, z: 4, core: 2. Of those that a mesh axis runs over, the one named last changes fastest.
Arguments:
- trailing: float32 [6144, 4096], P('row', 'col'), may hold values from -6 to 6
- column_block: bfloat16 [6144, 1024], P('row', 'col'), may hold values from -6 to 6
- row_block: bfloat16 [1024, 4096], P('row', 'col'), may hold values from -0.1875 to 0.1875
- lower_inv: bfloat16 [1024, 1024], replicated, may hold values from -1 to 1, as said below
- upper_inv: bfloat16 [1024, 1024], replicated, may hold values from -2 to 2, as said below
Outputs:
- lower_panel: bfloat16 [6144, 1024], P('row', 'col')
- upper_panel: bfloat16 [1024, 4096], P('row', 'col')
- updated: float32 [6144, 4096], P('row', 'col')
Inputs may be any that keep to these rules, and one draw needn't show every extreme that they name: `lower_inv`: lower triangular with ones on the diagonal. `upper_inv`: upper triangular with diagonal entries between 0.5 and 2.
All inputs are finite; a program needn't handle non-finite values.
Results may differ from a plain program's by a relative error of at most 0.0044.
Values may be sent and summed in bfloat16 or wider, within the bound.
A program may use at most 64 MiB of HBM per device.

v0:
```python
import functools

import jax
import jax.numpy as jnp
from jax import lax
from jax.experimental import pallas as pl
from jax.experimental.pallas import tpu as pltpu
from jax.sharding import PartitionSpec as P

MESH = pl.DeviceIdType.MESH
BLOCK = 256
PARTS = (3, 3, 3, 3)
ROW_CHUNKS = 4


def chunks_of(rows):
    unit = rows // sum(PARTS)
    starts = [sum(PARTS[:k]) * unit for k in range(len(PARTS))]
    return [(start, part * unit) for start, part in zip(starts, PARTS)]


def reach(size, chunk):
    each = (size - 1) // 2
    extra = 1 if size % 2 == 0 else 0
    return (each + extra, each) if chunk % 2 == 0 else (each, each + extra)


def kernel(
    n_row, n_col,
    trailing, column_block, row_block, lower_inv, upper_inv,
    lower_tile, lower_last, upper, updated,
    gathered, strips, linv, uinv, lower,
    local_sem, own_sem, col_send, col_recv, row_send, row_recv, sib_send, sib_recv, met,
):
    rows, share = column_block.shape
    depth, cols = row_block.shape
    order = lower_inv.shape[0]
    pieces = chunks_of(rows)
    wide = cols // ROW_CHUNKS
    row, col = lax.axis_index("row"), lax.axis_index("col")
    chips = n_row // 2
    half = chips // 2
    core = lax.rem(row, 2)

    def snake(place):
        return place + (place // half) * (chips + half - 1 - 2 * place)

    place = snake(row // 2)

    def chip_at(offset):
        return snake(lax.rem(place + chips + offset, chips))

    sibling = {"row": row + 1 - 2 * core}
    row_next = {"row": chip_at(1) * 2 + core}
    row_prev = {"row": chip_at(-1) * 2 + core}
    after = {"col": col + 1}
    before = {"col": col - 1}
    has_after = col < n_col - 1
    has_before = col > 0

    load_l = pltpu.make_async_copy(lower_inv, linv, local_sem.at[0])
    load_u = pltpu.make_async_copy(upper_inv, uinv, local_sem.at[1])
    load_t = pltpu.make_async_copy(trailing, updated, local_sem.at[2])
    mine_c = pltpu.make_async_copy(column_block, gathered.at[col], own_sem.at[0])
    my_rows = pl.ds(pl.multiple_of(row * depth, depth), depth)
    mine_r = pltpu.make_async_copy(row_block, strips.at[my_rows], own_sem.at[1])

    barrier = pltpu.get_barrier_semaphore()

    def greet(device):
        pl.semaphore_signal(barrier, inc=1, device_id=device, device_id_type=MESH)

    pl.when(has_after)(lambda: greet(after))
    pl.when(has_before)(lambda: greet(before))
    greet(row_next)
    greet(row_prev)
    pl.when(core == 0)(lambda: greet(sibling))
    mine_c.start()
    mine_r.start()
    load_l.start()
    load_u.start()
    ahead = (2 * n_col - 3 - col) // (n_col - 1)
    behind = (n_col - 2 + col) // (n_col - 1)
    pl.semaphore_wait(barrier, 2 + core + ahead + behind)

    @pl.when(core == 1)
    def _():
        pl.semaphore_signal(met, inc=1, device_id=sibling, device_id_type=MESH)


    sent = []

    def send(src, dst, send_sem, recv_sem, device):
        copy = pltpu.make_async_remote_copy(
            src_ref=src, dst_ref=dst, send_sem=send_sem, recv_sem=recv_sem,
            device_id=device, device_id_type=MESH,
        )
        copy.start()
        sent.append(copy)

    def arrived(dst, sem):
        pltpu.make_async_copy(dst, dst, sem).wait()

    def col_slot(owner, chunk):
        return gathered.at[owner, pl.ds(*pieces[chunk])]

    def col_copy(way, step, chunk):
        owner = col + (1 - step if way == 0 else step - 1)
        slot = col_slot(owner, chunk)
        return pltpu.make_async_remote_copy(
            src_ref=column_block.at[pl.ds(*pieces[chunk])] if step == 1 else slot,
            dst_ref=slot,
            send_sem=col_send.at[way, step - 1, chunk],
            recv_sem=col_recv.at[way, step - 1, chunk],
            device_id=after if way == 0 else before,
            device_id_type=MESH,
        )

    def sends(way, step):
        if way == 0:
            return has_after if step == 1 else has_after & (col >= step - 1)
        return has_before if step == 1 else has_before & (col + step - 1 < n_col)

    def takes(way, step):
        return col >= step if way == 0 else col + step < n_col

    def col_own(way):
        @pl.when(sends(way, 1))
        def _():
            for chunk in range(len(pieces)):
                col_copy(way, 1, chunk).start()

    def col_event(step, chunk):
        for way in range(2):
            @pl.when(takes(way, step))
            def _():
                slot = col_slot(col - step if way == 0 else col + step, chunk)
                arrived(slot, col_recv.at[way, step - 1, chunk])

            if step < n_col - 1:
                @pl.when(sends(way, step + 1))
                def _():
                    col_copy(way, step + 1, chunk).start()

    def col_drain():
        for way in range(2):
            for step in range(1, n_col):
                @pl.when(sends(way, step))
                def _():
                    for chunk in range(len(pieces)):
                        col_copy(way, step, chunk).wait_send()

    def strip(offset, lane, chunk):
        owner = chip_at(offset) * 2 + lane
        start = pl.multiple_of(owner * depth, depth)
        return strips.at[pl.ds(start, depth), pl.ds(chunk * wide, wide)]

    def row_send_to(way, step, chunk, src):
        offset = (1 - step) if way == 0 else (step - 1)
        send(
            src, strip(offset, core, chunk),
            row_send.at[way, step - 1, chunk], row_recv.at[way, step - 1, chunk],
            row_next if way == 0 else row_prev,
        )

    def share_strip(offset, chunk, src):
        at = offset + half
        send(
            src, strip(offset, core, chunk),
            sib_send.at[at, chunk], sib_recv.at[at, chunk], sibling,
        )

    shared = [[] for _ in range(ROW_CHUNKS)]

    def row_own(chunk):
        src = row_block.at[:, pl.ds(chunk * wide, wide)]
        for way in range(2):
            if reach(chips, chunk)[way] >= 1:
                row_send_to(way, 1, chunk, src)

    def row_event(step, chunk):
        for way in range(2):
            limit = reach(chips, chunk)[way]
            if step <= limit:
                offset = -step if way == 0 else step
                slot = strip(offset, core, chunk)
                arrived(slot, row_recv.at[way, step - 1, chunk])
                if step < limit:
                    row_send_to(way, step + 1, chunk, slot)
                share_strip(offset, chunk, slot)
                shared[chunk].append(offset)

    def row_shared(chunk):
        for offset in shared[chunk]:
            arrived(strip(offset, 1 - core, chunk), sib_recv.at[offset + half, chunk])

    def make_upper(chunk):
        at = pl.ds(chunk * wide, wide)
        for i in range(order // BLOCK):
            end = (i + 1) * BLOCK
            upper[pl.ds(i * BLOCK, BLOCK), at] = jnp.dot(
                linv[pl.ds(i * BLOCK, BLOCK), pl.ds(0, end)],
                strips[pl.ds(0, end), at],
                preferred_element_type=jnp.float32,
            ).astype(jnp.bfloat16)

    def make_lower(chunk):
        at = pl.ds(*pieces[chunk])
        parts = [gathered[k, at] for k in range(n_col)]
        left = jnp.concatenate(parts, axis=1)
        for j in range(order // BLOCK):
            end = (j + 1) * BLOCK
            lower[at, pl.ds(j * BLOCK, BLOCK)] = jnp.dot(
                left[:, :end],
                uinv[pl.ds(0, end), pl.ds(j * BLOCK, BLOCK)],
                preferred_element_type=jnp.float32,
            ).astype(jnp.bfloat16)
        if share % 128 == 0:
            lower_tile[at] = lower[at, pl.ds(pl.multiple_of(col * share, share), share)]
        else:
            for k in range(n_col):
                @pl.when(col == k)
                def _():
                    lower_tile[at] = lower[at, pl.ds(k * share, share)]
        if chunk == len(pieces) - 1:
            lower_last[...] = lower[at]

    def subtract(chunk):
        at = pl.ds(*pieces[chunk])
        updated[at] -= jnp.dot(lower[at], upper[...], preferred_element_type=jnp.float32)

    col_own(0)
    col_own(1)
    for chunk in range(ROW_CHUNKS):
        row_own(chunk)
    load_t.start()
    pl.when(core == 0)(lambda: pl.semaphore_wait(met, 1))
    for chunk in range(ROW_CHUNKS):
        share_strip(0, chunk, row_block.at[:, pl.ds(chunk * wide, wide)])
        shared[chunk].append(0)
    row_depth = max(max(reach(chips, r)) for r in range(ROW_CHUNKS))
    last = len(pieces) - 1
    for chunk in range(max(len(pieces), ROW_CHUNKS)):
        if chunk < ROW_CHUNKS:
            row_event(1, chunk)
        if chunk <= last:
            col_event(1, chunk)
    for step in range(2, row_depth + 1):
        for chunk in range(ROW_CHUNKS):
            row_event(step, chunk)
    mine_c.wait()
    mine_r.wait()
    load_l.wait()
    load_u.wait()
    for chunk in range(ROW_CHUNKS):
        row_shared(chunk)
        make_upper(chunk)
    load_t.wait()
    for step in range(2, n_col - 1):
        for chunk in range(len(pieces)):
            col_event(step, chunk)
    for chunk in range(len(pieces)):
        col_event(n_col - 1, chunk)
        if chunk == last:
            for copy in sent:
                copy.wait_send()
            col_drain()
        make_lower(chunk)
        if chunk < last:
            subtract(chunk)


def finish(lower_last, lower_done, upper, partial, lower_tile, upper_tile, updated, rest, sem):
    rows, cols = partial.shape
    depth = upper_tile.shape[0]
    start = pl.multiple_of(lax.axis_index("row") * depth, depth)
    pieces = chunks_of(rows)
    at = pl.ds(*pieces[-1])
    copies = [
        pltpu.make_async_copy(partial.at[pl.ds(*piece)], updated.at[pl.ds(*piece)], sem.at[k])
        for k, piece in enumerate(pieces[:-1])
    ]
    copies.append(pltpu.make_async_copy(lower_done, lower_tile, sem.at[len(pieces)]))
    copies.append(
        pltpu.make_async_copy(upper.at[pl.ds(start, depth)], upper_tile, sem.at[len(pieces) + 1])
    )
    for copy in copies:
        copy.start()
    for j in range(cols // BLOCK):
        across = pl.ds(j * BLOCK, BLOCK)
        rest[:, across] = partial[at, across] - jnp.dot(
            lower_last[...], upper[:, across], preferred_element_type=jnp.float32
        )
    tail = pltpu.make_async_copy(rest, updated.at[at], sem.at[len(pieces) - 1])
    tail.start()
    for copy in copies:
        copy.wait()
    tail.wait()


def on_device(n_row, n_col, trailing, column_block, row_block, lower_inv, upper_inv):
    rows, share = column_block.shape
    depth, cols = row_block.shape
    order = lower_inv.shape[0]
    chips = n_row // 2
    hops = chips // 2
    narrow = jnp.bfloat16
    hbm = pl.BlockSpec(memory_space=pltpu.HBM)
    inside = pl.BlockSpec(memory_space=pltpu.VMEM)
    dma = pltpu.SemaphoreType.DMA
    count = len(PARTS)
    last = chunks_of(rows)[-1][1]
    inputs = (trailing, column_block, row_block, lower_inv, upper_inv)
    tile = jax.ShapeDtypeStruct((rows, share), narrow)
    whole = jax.ShapeDtypeStruct((rows, cols), jnp.float32)
    lower_done, lower_last, upper, partial = pl.pallas_call(
        functools.partial(kernel, n_row, n_col),
        out_shape=(
            tile,
            jax.ShapeDtypeStruct((last, order), narrow),
            jax.ShapeDtypeStruct((order, cols), narrow),
            whole,
        ),
        in_specs=[hbm] * 5,
        out_specs=(inside,) * 4,
        scratch_shapes=[
            pltpu.VMEM((n_col, rows, share), narrow),
            pltpu.VMEM((order, cols), narrow),
            pltpu.VMEM((order, order), narrow),
            pltpu.VMEM((order, order), narrow),
            pltpu.VMEM((rows, order), narrow),
            dma((3,)),
            dma((2,)),
            dma((2, n_col - 1, count)),
            dma((2, n_col - 1, count)),
            dma((2, hops, ROW_CHUNKS)),
            dma((2, hops, ROW_CHUNKS)),
            dma((2 * hops + 1, ROW_CHUNKS)),
            dma((2 * hops + 1, ROW_CHUNKS)),
            pltpu.SemaphoreType.REGULAR,
        ],
        compiler_params=pltpu.CompilerParams(
            collective_id=0, has_side_effects=True, vmem_limit_bytes=32 << 20
        ),
    )(*(pltpu.with_memory_space_constraint(x, pltpu.HBM) for x in inputs))
    return pl.pallas_call(
        finish,
        out_shape=(tile, jax.ShapeDtypeStruct((depth, cols), narrow), whole),
        in_specs=[inside] * 4,
        out_specs=(hbm,) * 3,
        scratch_shapes=[pltpu.VMEM((last, cols), jnp.float32), dma((count + 2,))],
        compiler_params=pltpu.CompilerParams(vmem_limit_bytes=16 << 20),
    )(lower_last, lower_done, upper, partial)


def solution(mesh):
    specs = P("row", "col")
    return jax.shard_map(
        functools.partial(on_device, mesh.shape["row"], mesh.shape["col"]),
        mesh=mesh,
        in_specs=(specs, specs, specs, P(), P()),
        out_specs=(specs,) * 3,
        check_vma=False,
    )
```

profile of v0, /device:TPU:0, one launch (start us, length us, event | category | flops | bytes accessed | tf_op | source)
XLA Modules:
  0.0 34.9 jit_solution(4917100766334955458)
XLA Ops:
  0.6 32.3 %shard_map.76 = (bf16[768,256]{1,0:T(8,128)(2,1)S(1)}, bf16[192,1024]{1,0:T(8,128)(2,1)S(1)}, bf16[1024,1024]{1,0:T(8,128)(2,1)S(1)}, f32[768,1024]{1,0:T(8,128)S(1)}) custom-call(f32[768,1024]{1,0:T(8,128)} %trailing.1, bf16[768,256]{1,0:T(8,128)(2,1)} %column_block.1, bf16[128,1024]{1,0:T(8,128)(2,1)} %row_block.1, bf16[1024,1024]{1,0:T(8,128)(2,1)} %lower_inv.1, ...), custom_call_target="tpu_custom_call" | custom-call | tf_op jit(solution)/shard_map/pallas_call | solution.py:316
  33.0 1.9 %shard_map.77 = (bf16[768,256]{1,0:T(8,128)(2,1)}, bf16[128,1024]{1,0:T(8,128)(2,1)}, f32[768,1024]{1,0:T(8,128)}) custom-call(bf16[192,1024]{1,0:T(8,128)(2,1)S(1)} %get-tuple-element.7.lower_last, bf16[768,256]{1,0:T(8,128)(2,1)S(1)} %get-tuple-element.8.lower_done, bf16[1024,1024]{1,0:T(8,128)(2,1)S(1)} %get-tuple-element.9.upper, ...), custom_call_target="tpu_custom_call" | custom-call | tf_op jit(solution)/shard_map/pallas_call | solution.py:346
where the time goes:
time: 35.1 us; the launch traced here: 34.9 us
  Pallas kernels  34.3 us (98%)
  between operations  0.64 us (2%)
    pallas_call x1, Pallas kernels, on_device(): pl.pallas_call(functools.partial(kernel, n_row, n_col), out_shape=(tile,...  32.3 us
    pallas_call x1, Pallas kernels, on_device(): pl.pallas_call(finish, out_shape=(tile, jax.ShapeDtypeStruct((depth, cols...  1.93 us

commit v1 on v0

v1 whole, which is shorter than its diff:
```python
import functools

import jax
import jax.numpy as jnp
from jax import lax
from jax.experimental import pallas as pl
from jax.experimental.pallas import tpu as pltpu
from jax.sharding import PartitionSpec as P

MESH = pl.DeviceIdType.MESH
BLOCK = 256
PARTS = (3, 3, 2)
ROW_CHUNKS = 2


def chunks_of(rows):
    unit = rows // sum(PARTS)
    starts = [sum(PARTS[:k]) * unit for k in range(len(PARTS))]
    return [(start, part * unit) for start, part in zip(starts, PARTS)]


def reach(size, chunk):
    each = (size - 1) // 2
    extra = 1 if size % 2 == 0 else 0
    return (each + extra, each) if chunk % 2 == 0 else (each, each + extra)


def row_slots(chips):
    slots = {}
    for chunk in range(ROW_CHUNKS):
        for way, limit in enumerate(reach(chips, chunk)):
            for step in range(1, limit + 1):
                slots[way, step, chunk] = len(slots)
    return slots


def kernel(
    n_row, n_col,
    trailing, column_block, row_block, lower_inv, upper_inv,
    lower_tile, gathered, uinv, upper, updated,
    strips, linv, lower,
    local_sem, col_send, col_recv, row_send, row_recv, sib_recv, met,
):
    rows, share = column_block.shape
    depth, cols = row_block.shape
    order = lower_inv.shape[0]
    pieces = chunks_of(rows)
    wide = cols // ROW_CHUNKS
    row, col = lax.axis_index("row"), lax.axis_index("col")
    chips = n_row // 2
    half = chips // 2
    core = lax.rem(row, 2)

    def snake(place):
        return place + (place // half) * (chips + half - 1 - 2 * place)

    place = snake(row // 2)

    def chip_at(offset):
        return snake(lax.rem(place + chips + offset, chips))

    sibling = {"row": row + 1 - 2 * core}
    next_row = chip_at(1) * 2 + core
    prev_row = chip_at(-1) * 2 + core
    row_next = {"row": next_row}
    row_prev = {"row": prev_row}
    next_later = next_row > row
    prev_later = prev_row > row
    after = {"col": col + 1}
    before = {"col": col - 1}
    has_after = col < n_col - 1
    has_before = col > 0

    load_l = pltpu.make_async_copy(lower_inv, linv, local_sem.at[0])
    load_u = pltpu.make_async_copy(upper_inv, uinv, local_sem.at[1])
    load_t = pltpu.make_async_copy(trailing, updated, local_sem.at[2])
    mine_c = pltpu.make_async_copy(column_block, gathered.at[col], local_sem.at[3])
    my_rows = pl.ds(pl.multiple_of(row * depth, depth), depth)
    mine_r = pltpu.make_async_copy(row_block, strips.at[my_rows], local_sem.at[4])

    barrier = pltpu.get_barrier_semaphore()

    def greet(device):
        pl.semaphore_signal(barrier, inc=1, device_id=device, device_id_type=MESH)

    def reply(index, device):
        pl.semaphore_signal(met.at[index], inc=1, device_id=device, device_id_type=MESH)

    def await_reply(index):
        pl.semaphore_wait(met.at[index], 1)

    pl.when(has_after)(lambda: greet(after))
    pl.when(next_later)(lambda: greet(row_next))
    pl.when(prev_later)(lambda: greet(row_prev))
    pl.when(core == 0)(lambda: greet(sibling))
    mine_c.start()
    mine_r.start()
    load_l.start()
    load_u.start()
    behind = (col + n_col - 1) // n_col
    below = (row - next_row + n_row) // n_row + (row - prev_row + n_row) // n_row
    early = core + below + behind
    pl.when(early > 0)(lambda: pl.semaphore_wait(barrier, early))
    pl.when(has_before)(lambda: reply(0, before))
    pl.when(prev_row < row)(lambda: reply(1, row_prev))
    pl.when(next_row < row)(lambda: reply(2, row_next))
    pl.when(core == 1)(lambda: reply(3, sibling))

    slots = row_slots(chips)

    def send(src, dst, recv_sem, device):
        pltpu.make_async_remote_copy(
            src_ref=src, dst_ref=dst, send_sem=row_send, recv_sem=recv_sem,
            device_id=device, device_id_type=MESH,
        ).start()

    def arrived(dst, sem):
        pltpu.make_async_copy(dst, dst, sem).wait()

    def col_slot(owner, chunk):
        return gathered.at[owner, pl.ds(*pieces[chunk])]

    def col_copy(way, step, chunk):
        owner = col + (1 - step if way == 0 else step - 1)
        slot = col_slot(owner, chunk)
        straight = step == 1 and way == 1
        return pltpu.make_async_remote_copy(
            src_ref=column_block.at[pl.ds(*pieces[chunk])] if straight else slot,
            dst_ref=slot,
            send_sem=col_send.at[way],
            recv_sem=col_recv.at[owner - way, chunk],
            device_id=after if way == 0 else before,
            device_id_type=MESH,
        )

    def sends(way, step):
        if way == 0:
            return has_after if step == 1 else has_after & (col >= step - 1)
        return has_before if step == 1 else has_before & (col + step - 1 < n_col)

    def takes(way, step):
        return col >= step if way == 0 else col + step < n_col

    def col_own(way, lane):
        @pl.when(sends(way, 1) & (core == lane))
        def _():
            for chunk in range(len(pieces)):
                col_copy(way, 1, chunk).start()

    def col_event(step, chunk):
        for way in range(2):
            @pl.when(takes(way, step))
            def _():
                owner = col - step if way == 0 else col + step
                arrived(col_slot(owner, chunk), col_recv.at[owner - way, chunk])

            if step < n_col - 1:
                @pl.when(sends(way, step + 1))
                def _():
                    col_copy(way, step + 1, chunk).start()

    def drain():
        for count in range(1, n_col):
            block = gathered.at[pl.ds(0, count)]
            pl.when(col + 1 == count)(lambda: arrived(block, col_send.at[0]))
            pl.when(n_col - col == count)(lambda: arrived(block, col_send.at[1]))
        arrived(strips.at[pl.ds(0, (n_row - 1) * depth)], row_send)

    def strip(offset, lane, chunk):
        owner = chip_at(offset) * 2 + lane
        start = pl.multiple_of(owner * depth, depth)
        return strips.at[pl.ds(start, depth), pl.ds(chunk * wide, wide)]

    def row_send_to(way, step, chunk, src):
        offset = (1 - step) if way == 0 else (step - 1)
        send(
            src, strip(offset, core, chunk),
            row_recv.at[slots[way, step, chunk]],
            row_next if way == 0 else row_prev,
        )

    def share_strip(offset, chunk, src):
        send(src, strip(offset, core, chunk), sib_recv.at[chunk], sibling)

    def row_own(chunk):
        src = row_block.at[:, pl.ds(chunk * wide, wide)]
        for way in range(2):
            if reach(chips, chunk)[way] >= 1:
                row_send_to(way, 1, chunk, src)

    def row_event(step, chunk):
        for way in range(2):
            limit = reach(chips, chunk)[way]
            if step <= limit:
                offset = -step if way == 0 else step
                slot = strip(offset, core, chunk)
                arrived(slot, row_recv.at[slots[way, step, chunk]])
                if step < limit:
                    row_send_to(way, step + 1, chunk, slot)
                share_strip(offset, chunk, slot)

    def row_shared(chunk):
        block = strips.at[pl.ds(0, chips * depth), pl.ds(chunk * wide, wide)]
        arrived(block, sib_recv.at[chunk])

    def make_upper(chunk):
        at = pl.ds(chunk * wide, wide)
        for i in range(order // BLOCK):
            end = (i + 1) * BLOCK
            upper[pl.ds(i * BLOCK, BLOCK), at] = jnp.dot(
                linv[pl.ds(i * BLOCK, BLOCK), pl.ds(0, end)],
                strips[pl.ds(0, end), at],
                preferred_element_type=jnp.float32,
            ).astype(jnp.bfloat16)

    def make_lower(chunk):
        at = pl.ds(*pieces[chunk])
        parts = [gathered[k, at] for k in range(n_col)]
        left = jnp.concatenate(parts, axis=1)
        for j in range(order // BLOCK):
            end = (j + 1) * BLOCK
            lower[at, pl.ds(j * BLOCK, BLOCK)] = jnp.dot(
                left[:, :end],
                uinv[pl.ds(0, end), pl.ds(j * BLOCK, BLOCK)],
                preferred_element_type=jnp.float32,
            ).astype(jnp.bfloat16)
        if share % 128 == 0:
            lower_tile[at] = lower[at, pl.ds(pl.multiple_of(col * share, share), share)]
        else:
            for k in range(n_col):
                @pl.when(col == k)
                def _():
                    lower_tile[at] = lower[at, pl.ds(k * share, share)]

    def subtract(chunk):
        at = pl.ds(*pieces[chunk])
        updated[at] -= jnp.dot(lower[at], upper[...], preferred_element_type=jnp.float32)

    col_own(1, 0)
    mine_c.wait()
    pl.when(has_after)(lambda: await_reply(0))
    col_own(0, 0)
    pl.when(next_later)(lambda: await_reply(1))
    pl.when(prev_later)(lambda: await_reply(2))
    for chunk in range(ROW_CHUNKS):
        row_own(chunk)
    load_l.wait()
    col_own(1, 1)
    col_own(0, 1)
    load_t.start()
    pl.when(core == 0)(lambda: await_reply(3))
    for chunk in range(ROW_CHUNKS):
        share_strip(0, chunk, row_block.at[:, pl.ds(chunk * wide, wide)])
    row_depth = max(max(reach(chips, r)) for r in range(ROW_CHUNKS))
    last = len(pieces) - 1
    for chunk in range(max(len(pieces), ROW_CHUNKS)):
        if chunk < ROW_CHUNKS:
            row_event(1, chunk)
        if chunk <= last:
            col_event(1, chunk)
    for step in range(2, row_depth + 1):
        for chunk in range(ROW_CHUNKS):
            row_event(step, chunk)
    mine_r.wait()
    load_u.wait()
    for chunk in range(ROW_CHUNKS):
        row_shared(chunk)
        make_upper(chunk)
    load_t.wait()
    for step in range(2, n_col - 1):
        for chunk in range(len(pieces)):
            col_event(step, chunk)
    for chunk in range(len(pieces)):
        col_event(n_col - 1, chunk)
        if chunk < last:
            make_lower(chunk)
            subtract(chunk)
    drain()


def finish(
    n_col, lower_done, gathered, uinv, upper, partial, lower_tile, upper_tile, updated,
    low, tile, rest, sem,
):
    rows, cols = partial.shape
    share = lower_tile.shape[1]
    depth = upper_tile.shape[0]
    order = uinv.shape[0]
    col = lax.axis_index("col")
    start = pl.multiple_of(lax.axis_index("row") * depth, depth)
    begin, size = chunks_of(rows)[-1]
    at, done = pl.ds(begin, size), pl.ds(0, begin)
    copies = []

    def copy(src, dst):
        copies.append(pltpu.make_async_copy(src, dst, sem.at[len(copies)]))
        copies[-1].start()

    copy(partial.at[done], updated.at[done])
    copy(lower_done.at[done], lower_tile.at[done])
    copy(upper.at[pl.ds(start, depth)], upper_tile)
    left = jnp.concatenate([gathered[k, at] for k in range(n_col)], axis=1)
    for j in range(order // BLOCK):
        end = (j + 1) * BLOCK
        low[:, pl.ds(j * BLOCK, BLOCK)] = jnp.dot(
            left[:, :end],
            uinv[pl.ds(0, end), pl.ds(j * BLOCK, BLOCK)],
            preferred_element_type=jnp.float32,
        ).astype(jnp.bfloat16)
    if share % 128 == 0:
        tile[...] = low[:, pl.ds(pl.multiple_of(col * share, share), share)]
    else:
        for k in range(n_col):
            @pl.when(col == k)
            def _():
                tile[...] = low[:, pl.ds(k * share, share)]
    copy(tile, lower_tile.at[at])
    for j in range(cols // BLOCK):
        across = pl.ds(j * BLOCK, BLOCK)
        rest[:, across] = partial[at, across] - jnp.dot(
            low[...], upper[:, across], preferred_element_type=jnp.float32
        )
        copy(rest.at[:, across], updated.at[at, across])
    for each in copies:
        each.wait()


def on_device(n_row, n_col, trailing, column_block, row_block, lower_inv, upper_inv):
    rows, share = column_block.shape
    depth, cols = row_block.shape
    order = lower_inv.shape[0]
    chips = n_row // 2
    narrow = jnp.bfloat16
    hbm = pl.BlockSpec(memory_space=pltpu.HBM)
    inside = pl.BlockSpec(memory_space=pltpu.VMEM)
    dma = pltpu.SemaphoreType.DMA
    count = len(PARTS)
    last = chunks_of(rows)[-1][1]
    inputs = (trailing, column_block, row_block, lower_inv, upper_inv)
    tile = jax.ShapeDtypeStruct((rows, share), narrow)
    whole = jax.ShapeDtypeStruct((rows, cols), jnp.float32)
    lower_done, gathered, uinv, upper, partial = pl.pallas_call(
        functools.partial(kernel, n_row, n_col),
        out_shape=(
            tile,
            jax.ShapeDtypeStruct((n_col, rows, share), narrow),
            jax.ShapeDtypeStruct((order, order), narrow),
            jax.ShapeDtypeStruct((order, cols), narrow),
            whole,
        ),
        in_specs=[hbm] * 5,
        out_specs=(inside,) * 5,
        scratch_shapes=[
            pltpu.VMEM((order, cols), narrow),
            pltpu.VMEM((order, order), narrow),
            pltpu.VMEM((rows, order), narrow),
            dma((5,)),
            dma((2,)),
            dma((n_col - 1, count)),
            dma,
            dma((len(row_slots(chips)),)),
            dma((ROW_CHUNKS,)),
            pltpu.SemaphoreType.REGULAR((4,)),
        ],
        compiler_params=pltpu.CompilerParams(
            collective_id=0, has_side_effects=True, vmem_limit_bytes=32 << 20
        ),
    )(*(pltpu.with_memory_space_constraint(x, pltpu.HBM) for x in inputs))
    return pl.pallas_call(
        functools.partial(finish, n_col),
        out_shape=(tile, jax.ShapeDtypeStruct((depth, cols), narrow), whole),
        in_specs=[inside] * 5,
        out_specs=(hbm,) * 3,
        scratch_shapes=[
            pltpu.VMEM((last, order), narrow),
            pltpu.VMEM((last, share), narrow),
            pltpu.VMEM((last, cols), jnp.float32),
            dma((4 + cols // BLOCK,)),
        ],
        compiler_params=pltpu.CompilerParams(vmem_limit_bytes=16 << 20),
    )(lower_done, gathered, uinv, upper, partial)


def solution(mesh):
    specs = P("row", "col")
    return jax.shard_map(
        functools.partial(on_device, mesh.shape["row"], mesh.shape["col"]),
        mesh=mesh,
        in_specs=(specs, specs, specs, P(), P()),
        out_specs=(specs,) * 3,
        check_vma=False,
    )
```

time: 35.1 us -> 32.7 us (0.932)
  Pallas kernels: 34.3 us -> 31.9 us
    pallas_call x1, Pallas kernels: 32.3 us -> 30 us  [on_device(): pl.pallas_call(functools.partial(kernel, n_row, n_col), out_shape=(tile,...]
where the time goes in v1:
time: 32.7 us; the launch traced here: 32.6 us
  Pallas kernels  31.9 us (98%)
  between operations  0.64 us (2%)
    pallas_call x1, Pallas kernels, on_device(): pl.pallas_call(functools.partial(kernel, n_row, n_col), out_shape=(tile,...  30 us
    pallas_call x1, Pallas kernels, on_device(): pl.pallas_call(functools.partial(finish, n_col), out_shape=(tile, jax.Sha...  1.93 us

profile of v1, /device:TPU:0, one launch (start us, length us, event | category | flops | bytes accessed | tf_op | source)
XLA Modules:
  0.0 32.6 jit_solution(11630377584594536939)
XLA Ops:
  0.6 30.0 %shard_map.76 = (bf16[768,256]{1,0:T(8,128)(2,1)S(1)}, bf16[4,768,256]{2,1,0:T(8,128)(2,1)S(1)}, bf16[1024,1024]{1,0:T(8,128)(2,1)S(1)}, bf16[1024,1024]{1,0:T(8,128)(2,1)S(1)}, f32[768,1024]{1,0:T(8,128)S(1)}) custom-call(f32[768,1024]{1,0:T(8,128)} %trailing.1, bf16[768,256]{1,0:T(8,128)(2,1)} %column_block.1, bf16[128,1024]{1,0:T(8,128)(2,1)} %row_block.1, ...), custom_call_target="tpu_custom_call" | custom-call | tf_op jit(solution)/shard_map/pallas_call | solution.py:342
  30.6 1.9 %shard_map.77 = (bf16[768,256]{1,0:T(8,128)(2,1)}, bf16[128,1024]{1,0:T(8,128)(2,1)}, f32[768,1024]{1,0:T(8,128)}) custom-call(bf16[768,256]{1,0:T(8,128)(2,1)S(1)} %get-tuple-element.8.lower_done, bf16[4,768,256]{2,1,0:T(8,128)(2,1)S(1)} %get-tuple-element.9.gathered, bf16[1024,1024]{1,0:T(8,128)(2,1)S(1)} %get-tuple-element.10.uinv, ...), custom_call_target="tpu_custom_call" | custom-call | tf_op jit(solution)/shard_map/pallas_call | solution.py:369

commit v2 on v1

--- a/solution.py
+++ b/solution.py
@@ -11,6 +11,7 @@
 BLOCK = 256
 PARTS = (3, 3, 2)
 ROW_CHUNKS = 2
+DETOUR = 16
 
 
 def chunks_of(rows):
@@ -38,8 +39,8 @@
     n_row, n_col,
     trailing, column_block, row_block, lower_inv, upper_inv,
     lower_tile, gathered, uinv, upper, updated,
-    strips, linv, lower,
-    local_sem, col_send, col_recv, row_send, row_recv, sib_recv, met,
+    strips, linv, lower, spare,
+    local_sem, col_send, col_recv, row_send, row_recv, sib_recv, spare_send, spare_recv, met,
 ):
     rows, share = column_block.shape
     depth, cols = row_block.shape
@@ -117,15 +118,21 @@
     def arrived(dst, sem):
         pltpu.make_async_copy(dst, dst, sem).wait()
 
-    def col_slot(owner, chunk):
-        return gathered.at[owner, pl.ds(*pieces[chunk])]
-
-    def col_copy(way, step, chunk):
+    turn = rows // DETOUR
+
+    def span(chunk, short):
+        start, size = pieces[chunk]
+        return pl.ds(start, size - 2 * turn if short else size)
+
+    def col_slot(owner, chunk, short=False):
+        return gathered.at[owner, span(chunk, short)]
+
+    def col_copy(way, step, chunk, short=False):
         owner = col + (1 - step if way == 0 else step - 1)
-        slot = col_slot(owner, chunk)
+        slot = col_slot(owner, chunk, short)
         straight = step == 1 and way == 1
         return pltpu.make_async_remote_copy(
-            src_ref=column_block.at[pl.ds(*pieces[chunk])] if straight else slot,
+            src_ref=column_block.at[span(chunk, short)] if straight else slot,
             dst_ref=slot,
             send_sem=col_send.at[way],
             recv_sem=col_recv.at[owner - way, chunk],
@@ -141,18 +148,57 @@
     def takes(way, step):
         return col >= step if way == 0 else col + step < n_col
 
-    def col_own(way, lane):
-        @pl.when(sends(way, 1) & (core == lane))
+    def col_own(way):
+        for short in range(1 + way):
+            @pl.when(sends(way, 1) & turns(1, short) if way else sends(way, 1))
+            def _():
+                for chunk in range(len(pieces)):
+                    col_copy(way, 1, chunk, short and chunk == 0).start()
+
+    def turns(at, short):
+        here = (place == 0) & (col == at)
+        return here if short else (place != 0) | (col != at)
+
+    def turned(side):
+        return pl.ds(pieces[0][1] - (2 - side) * turn, turn)
+
+    def turning(side):
+        return (place == (chips - 1 if side else 1)) & (col == 1)
+
+    def turn_own():
+        @pl.when(turns(1, True))
         def _():
-            for chunk in range(len(pieces)):
-                col_copy(way, 1, chunk).start()
+            for side in range(2):
+                pltpu.make_async_remote_copy(
+                    src_ref=column_block.at[turned(side)], dst_ref=spare.at[side],
+                    send_sem=col_send.at[1], recv_sem=spare_recv.at[side],
+                    device_id=row_prev if side else row_next, device_id_type=MESH,
+                ).start()
+
+    def turn_event(side):
+        @pl.when(turning(side))
+        def _():
+            arrived(spare.at[side], spare_recv.at[side])
+            pltpu.make_async_remote_copy(
+                src_ref=spare.at[side], dst_ref=gathered.at[1, turned(side)],
+                send_sem=spare_send.at[side], recv_sem=spare_recv.at[side],
+                device_id={"row": next_row if side else prev_row, "col": col - 1},
+                device_id_type=MESH,
+            ).start()
+
+    def turn_last(side):
+        @pl.when(turns(0, True))
+        def _():
+            arrived(gathered.at[1, turned(side)], spare_recv.at[side])
 
     def col_event(step, chunk):
         for way in range(2):
-            @pl.when(takes(way, step))
-            def _():
-                owner = col - step if way == 0 else col + step
-                arrived(col_slot(owner, chunk), col_recv.at[owner - way, chunk])
+            cut = way == 1 and step == 1 and chunk == 0
+            for short in range(1 + cut):
+                @pl.when(takes(way, step) & turns(0, short) if cut else takes(way, step))
+                def _():
+                    owner = col - step if way == 0 else col + step
+                    arrived(col_slot(owner, chunk, short), col_recv.at[owner - way, chunk])
 
             if step < n_col - 1:
                 @pl.when(sends(way, step + 1))
@@ -165,6 +211,8 @@
             pl.when(col + 1 == count)(lambda: arrived(block, col_send.at[0]))
             pl.when(n_col - col == count)(lambda: arrived(block, col_send.at[1]))
         arrived(strips.at[pl.ds(0, (n_row - 1) * depth)], row_send)
+        for side in range(2):
+            pl.when(turning(side))(lambda: arrived(spare.at[side], spare_send.at[side]))
 
     def strip(offset, lane, chunk):
         owner = chip_at(offset) * 2 + lane
@@ -204,6 +252,7 @@
         arrived(block, sib_recv.at[chunk])
 
     def make_upper(chunk):
+        row_shared(chunk)
         at = pl.ds(chunk * wide, wide)
         for i in range(order // BLOCK):
             end = (i + 1) * BLOCK
@@ -236,17 +285,15 @@
         at = pl.ds(*pieces[chunk])
         updated[at] -= jnp.dot(lower[at], upper[...], preferred_element_type=jnp.float32)
 
-    col_own(1, 0)
+    col_own(1)
     mine_c.wait()
     pl.when(has_after)(lambda: await_reply(0))
-    col_own(0, 0)
+    col_own(0)
     pl.when(next_later)(lambda: await_reply(1))
     pl.when(prev_later)(lambda: await_reply(2))
+    turn_own()
     for chunk in range(ROW_CHUNKS):
         row_own(chunk)
-    load_l.wait()
-    col_own(1, 1)
-    col_own(0, 1)
     load_t.start()
     pl.when(core == 0)(lambda: await_reply(3))
     for chunk in range(ROW_CHUNKS):
@@ -258,18 +305,25 @@
             row_event(1, chunk)
         if chunk <= last:
             col_event(1, chunk)
+    for side in range(2):
+        turn_event(side)
     for step in range(2, row_depth + 1):
         for chunk in range(ROW_CHUNKS):
             row_event(step, chunk)
     mine_r.wait()
+    load_l.wait()
     load_u.wait()
-    for chunk in range(ROW_CHUNKS):
-        row_shared(chunk)
-        make_upper(chunk)
-    load_t.wait()
+    waiting = list(range(ROW_CHUNKS))
     for step in range(2, n_col - 1):
         for chunk in range(len(pieces)):
             col_event(step, chunk)
+            if step == n_col - 2 and waiting:
+                make_upper(waiting.pop(0))
+    for chunk in waiting:
+        make_upper(chunk)
+    load_t.wait()
+    for side in range(2):
+        turn_last(side)
     for chunk in range(len(pieces)):
         col_event(n_col - 1, chunk)
         if chunk < last:
@@ -354,12 +408,15 @@
             pltpu.VMEM((order, cols), narrow),
             pltpu.VMEM((order, order), narrow),
             pltpu.VMEM((rows, order), narrow),
+            pltpu.VMEM((2, rows // DETOUR, share), narrow),
             dma((5,)),
             dma((2,)),
             dma((n_col - 1, count)),
             dma,
             dma((len(row_slots(chips)),)),
             dma((ROW_CHUNKS,)),
+            dma((2,)),
+            dma((2,)),
             pltpu.SemaphoreType.REGULAR((4,)),
         ],
         compiler_params=pltpu.CompilerParams(

time: 32.7 us -> 32.1 us (0.982)
  Pallas kernels: 31.9 us -> 31.2 us
    pallas_call x1, Pallas kernels: 30 us -> 29.3 us  [on_device(): pl.pallas_call(functools.partial(kernel, n_row, n_col), out_shape=(tile,...]
where the time goes in v2:
time: 32.1 us; the launch traced here: 31.8 us
  Pallas kernels  31.2 us (97%)
  between operations  0.64 us (2%)
    pallas_call x1, Pallas kernels, on_device(): pl.pallas_call(functools.partial(kernel, n_row, n_col), out_shape=(tile,...  29.3 us
    pallas_call x1, Pallas kernels, on_device(): pl.pallas_call(functools.partial(finish, n_col), out_shape=(tile, jax.Sha...  1.93 us

profile of v2, /device:TPU:0, one launch (start us, length us, event | category | flops | bytes accessed | tf_op | source)
XLA Modules:
  0.0 31.8 jit_solution(11239543237963079333)
XLA Ops:
  0.6 29.3 %shard_map.76 = (bf16[768,256]{1,0:T(8,128)(2,1)S(1)}, bf16[4,768,256]{2,1,0:T(8,128)(2,1)S(1)}, bf16[1024,1024]{1,0:T(8,128)(2,1)S(1)}, bf16[1024,1024]{1,0:T(8,128)(2,1)S(1)}, f32[768,1024]{1,0:T(8,128)S(1)}) custom-call(f32[768,1024]{1,0:T(8,128)} %trailing.1, bf16[768,256]{1,0:T(8,128)(2,1)} %column_block.1, bf16[128,1024]{1,0:T(8,128)(2,1)} %row_block.1, ...), custom_call_target="tpu_custom_call" | custom-call | tf_op jit(solution)/shard_map/pallas_call | solution.py:396
  29.9 1.9 %shard_map.77 = (bf16[768,256]{1,0:T(8,128)(2,1)}, bf16[128,1024]{1,0:T(8,128)(2,1)}, f32[768,1024]{1,0:T(8,128)}) custom-call(bf16[768,256]{1,0:T(8,128)(2,1)S(1)} %get-tuple-element.8.lower_done, bf16[4,768,256]{2,1,0:T(8,128)(2,1)S(1)} %get-tuple-element.9.gathered, bf16[1024,1024]{1,0:T(8,128)(2,1)S(1)} %get-tuple-element.10.uinv, ...), custom_call_target="tpu_custom_call" | custom-call | tf_op jit(solution)/shard_map/pallas_call | solution.py:426

commit v3 on v2

--- a/solution.py
+++ b/solution.py
@@ -84,6 +84,9 @@
     def greet(device):
         pl.semaphore_signal(barrier, inc=1, device_id=device, device_id_type=MESH)
 
+    odd = lax.rem(col, 2)
+    even = odd == 0
+
     def reply(index, device):
         pl.semaphore_signal(met.at[index], inc=1, device_id=device, device_id_type=MESH)
 
@@ -91,21 +94,18 @@
         pl.semaphore_wait(met.at[index], 1)
 
     pl.when(has_after)(lambda: greet(after))
-    pl.when(next_later)(lambda: greet(row_next))
-    pl.when(prev_later)(lambda: greet(row_prev))
-    pl.when(core == 0)(lambda: greet(sibling))
+    pl.when(even & next_later)(lambda: greet(row_next))
+    pl.when(even & prev_later)(lambda: greet(row_prev))
+    pl.when(even & (core == 0))(lambda: greet(sibling))
     mine_c.start()
     mine_r.start()
     load_l.start()
     load_u.start()
     behind = (col + n_col - 1) // n_col
     below = (row - next_row + n_row) // n_row + (row - prev_row + n_row) // n_row
-    early = core + below + behind
+    early = behind + (core + below) * (1 - odd)
     pl.when(early > 0)(lambda: pl.semaphore_wait(barrier, early))
     pl.when(has_before)(lambda: reply(0, before))
-    pl.when(prev_row < row)(lambda: reply(1, row_prev))
-    pl.when(next_row < row)(lambda: reply(2, row_next))
-    pl.when(core == 1)(lambda: reply(3, sibling))
 
     slots = row_slots(chips)
 
@@ -191,17 +191,18 @@
         def _():
             arrived(gathered.at[1, turned(side)], spare_recv.at[side])
 
-    def col_event(step, chunk):
+    def col_event(step, chunk, lane=None):
+        mine = (core >= 0) if lane is None else (core == lane)
         for way in range(2):
             cut = way == 1 and step == 1 and chunk == 0
             for short in range(1 + cut):
-                @pl.when(takes(way, step) & turns(0, short) if cut else takes(way, step))
+                @pl.when(mine & (takes(way, step) & turns(0, short) if cut else takes(way, step)))
                 def _():
                     owner = col - step if way == 0 else col + step
                     arrived(col_slot(owner, chunk, short), col_recv.at[owner - way, chunk])
 
             if step < n_col - 1:
-                @pl.when(sends(way, step + 1))
+                @pl.when(mine & sends(way, step + 1))
                 def _():
                     col_copy(way, step + 1, chunk).start()
 
@@ -286,50 +287,70 @@
         updated[at] -= jnp.dot(lower[at], upper[...], preferred_element_type=jnp.float32)
 
     col_own(1)
+    pl.when(even & (prev_row < row))(lambda: reply(1, row_prev))
+    pl.when(even & (next_row < row))(lambda: reply(1, row_next))
+    pl.when(even & (core == 1))(lambda: reply(1, sibling))
     mine_c.wait()
     pl.when(has_after)(lambda: await_reply(0))
     col_own(0)
-    pl.when(next_later)(lambda: await_reply(1))
-    pl.when(prev_later)(lambda: await_reply(2))
+    late = (3 - core - below) * (1 - odd)
+    pl.when(late > 0)(lambda: pl.semaphore_wait(met.at[1], late))
+
+    @pl.when(even & has_after)
+    def _():
+        for device in (row_next, row_prev, sibling):
+            reply(2, device)
+
+    pl.when(odd == 1)(lambda: await_reply(3))
     turn_own()
     for chunk in range(ROW_CHUNKS):
         row_own(chunk)
     load_t.start()
-    pl.when(core == 0)(lambda: await_reply(3))
     for chunk in range(ROW_CHUNKS):
         share_strip(0, chunk, row_block.at[:, pl.ds(chunk * wide, wide)])
+
+    @pl.when(even & has_after)
+    def _():
+        pl.semaphore_wait(met.at[2], 3)
+        reply(3, after)
+
     row_depth = max(max(reach(chips, r)) for r in range(ROW_CHUNKS))
     last = len(pieces) - 1
-    for chunk in range(max(len(pieces), ROW_CHUNKS)):
-        if chunk < ROW_CHUNKS:
-            row_event(1, chunk)
-        if chunk <= last:
-            col_event(1, chunk)
+    row_left = [(step, r) for step in range(1, row_depth + 1) for r in range(ROW_CHUNKS)]
+    col_left = [(step, k) for step in range(2, n_col - 1) for k in range(len(pieces))]
+    col_event(1, 0, 0)
+    row_event(*row_left.pop(0))
+    col_event(1, 1)
+    col_event(1, 0, 1)
+    for chunk in range(2, len(pieces)):
+        col_event(1, chunk)
+    while row_left and row_left[0][0] == 1:
+        row_event(*row_left.pop(0))
     for side in range(2):
         turn_event(side)
-    for step in range(2, row_depth + 1):
-        for chunk in range(ROW_CHUNKS):
-            row_event(step, chunk)
+    while row_left:
+        row_event(*row_left.pop(0))
+        if col_left:
+            col_event(*col_left.pop(0))
     mine_r.wait()
     load_l.wait()
     load_u.wait()
-    waiting = list(range(ROW_CHUNKS))
-    for step in range(2, n_col - 1):
-        for chunk in range(len(pieces)):
-            col_event(step, chunk)
-            if step == n_col - 2 and waiting:
-                make_upper(waiting.pop(0))
-    for chunk in waiting:
+    for chunk in range(ROW_CHUNKS):
         make_upper(chunk)
+        if col_left:
+            col_event(*col_left.pop(0))
+    for step, chunk in col_left:
+        col_event(step, chunk)
     load_t.wait()
     for side in range(2):
         turn_last(side)
     for chunk in range(len(pieces)):
+        if chunk == last:
+            drain()
         col_event(n_col - 1, chunk)
         if chunk < last:
             make_lower(chunk)
             subtract(chunk)
-    drain()
 
 
 def finish(
@@ -344,15 +365,13 @@
     start = pl.multiple_of(lax.axis_index("row") * depth, depth)
     begin, size = chunks_of(rows)[-1]
     at, done = pl.ds(begin, size), pl.ds(0, begin)
-    copies = []
-
-    def copy(src, dst):
-        copies.append(pltpu.make_async_copy(src, dst, sem.at[len(copies)]))
-        copies[-1].start()
-
-    copy(partial.at[done], updated.at[done])
-    copy(lower_done.at[done], lower_tile.at[done])
-    copy(upper.at[pl.ds(start, depth)], upper_tile)
+
+    def copy(index, src, dst):
+        pltpu.make_async_copy(src, dst, sem.at[index]).start()
+
+    copy(0, partial.at[done], updated.at[done])
+    copy(1, lower_done.at[done], lower_tile.at[done])
+    copy(2, upper.at[pl.ds(start, depth)], upper_tile)
     left = jnp.concatenate([gathered[k, at] for k in range(n_col)], axis=1)
     for j in range(order // BLOCK):
         end = (j + 1) * BLOCK
@@ -368,15 +387,15 @@
             @pl.when(col == k)
             def _():
                 tile[...] = low[:, pl.ds(k * share, share)]
-    copy(tile, lower_tile.at[at])
+    copy(1, tile, lower_tile.at[at])
     for j in range(cols // BLOCK):
         across = pl.ds(j * BLOCK, BLOCK)
         rest[:, across] = partial[at, across] - jnp.dot(
             low[...], upper[:, across], preferred_element_type=jnp.float32
         )
-        copy(rest.at[:, across], updated.at[at, across])
-    for each in copies:
-        each.wait()
+        copy(0, rest.at[:, across], updated.at[at, across])
+    for index, whole in enumerate((updated, lower_tile, upper_tile)):
+        pltpu.make_async_copy(whole, whole, sem.at[index]).wait()
 
 
 def on_device(n_row, n_col, trailing, column_block, row_block, lower_inv, upper_inv):
@@ -432,7 +451,7 @@
             pltpu.VMEM((last, order), narrow),
             pltpu.VMEM((last, share), narrow),
             pltpu.VMEM((last, cols), jnp.float32),
-            dma((4 + cols // BLOCK,)),
+            dma((3,)),
         ],
         compiler_params=pltpu.CompilerParams(vmem_limit_bytes=16 << 20),
     )(lower_done, gathered, uinv, upper, partial)

time: 32.1 us -> 31.5 us (0.981)
  Pallas kernels: 31.2 us -> 30.5 us
    pallas_call x1, Pallas kernels: 29.3 us -> 28.6 us  [on_device(): pl.pallas_call(functools.partial(kernel, n_row, n_col), out_shape=(tile,...]
where the time goes in v3:
time: 31.5 us; the launch traced here: 31.2 us
  Pallas kernels  30.5 us (97%)
  between operations  0.64 us (2%)
    pallas_call x1, Pallas kernels, on_device(): pl.pallas_call(functools.partial(kernel, n_row, n_col), out_shape=(tile,...  28.6 us
    pallas_call x1, Pallas kernels, on_device(): pl.pallas_call(functools.partial(finish, n_col), out_shape=(tile, jax.Sha...  1.89 us

profile of v3, /device:TPU:0, one launch (start us, length us, event | category | flops | bytes accessed | tf_op | source)
XLA Modules:
  0.0 31.2 jit_solution(10771200511333755566)
XLA Ops:
  0.6 28.6 %shard_map.76 = (bf16[768,256]{1,0:T(8,128)(2,1)S(1)}, bf16[4,768,256]{2,1,0:T(8,128)(2,1)S(1)}, bf16[1024,1024]{1,0:T(8,128)(2,1)S(1)}, bf16[1024,1024]{1,0:T(8,128)(2,1)S(1)}, f32[768,1024]{1,0:T(8,128)S(1)}) custom-call(f32[768,1024]{1,0:T(8,128)} %trailing.1, bf16[768,256]{1,0:T(8,128)(2,1)} %column_block.1, bf16[128,1024]{1,0:T(8,128)(2,1)} %row_block.1, ...), custom_call_target="tpu_custom_call" | custom-call | tf_op jit(solution)/shard_map/pallas_call | solution.py:415
  29.3 1.9 %shard_map.77 = (bf16[768,256]{1,0:T(8,128)(2,1)}, bf16[128,1024]{1,0:T(8,128)(2,1)}, f32[768,1024]{1,0:T(8,128)}) custom-call(bf16[768,256]{1,0:T(8,128)(2,1)S(1)} %get-tuple-element.8.lower_done, bf16[4,768,256]{2,1,0:T(8,128)(2,1)S(1)} %get-tuple-element.9.gathered, bf16[1024,1024]{1,0:T(8,128)(2,1)S(1)} %get-tuple-element.10.uinv, ...), custom_call_target="tpu_custom_call" | custom-call | tf_op jit(solution)/shard_map/pallas_call | solution.py:445

commit v4 on v3

--- a/solution.py
+++ b/solution.py
@@ -26,13 +26,8 @@
     return (each + extra, each) if chunk % 2 == 0 else (each, each + extra)
 
 
-def row_slots(chips):
-    slots = {}
-    for chunk in range(ROW_CHUNKS):
-        for way, limit in enumerate(reach(chips, chunk)):
-            for step in range(1, limit + 1):
-                slots[way, step, chunk] = len(slots)
-    return slots
+def strips_due(chips, step):
+    return sum(limit >= step for r in range(ROW_CHUNKS) for limit in reach(chips, r))
 
 
 def kernel(
@@ -86,6 +81,8 @@
 
     odd = lax.rem(col, 2)
     even = odd == 0
+    held = even & (core == 1)
+    free = (odd == 1) | (core == 0)
 
     def reply(index, device):
         pl.semaphore_signal(met.at[index], inc=1, device_id=device, device_id_type=MESH)
@@ -99,7 +96,7 @@
     pl.when(even & (core == 0))(lambda: greet(sibling))
     mine_c.start()
     mine_r.start()
-    load_l.start()
+    pl.when(free)(lambda: load_l.start())
     load_u.start()
     behind = (col + n_col - 1) // n_col
     below = (row - next_row + n_row) // n_row + (row - prev_row + n_row) // n_row
@@ -107,7 +104,6 @@
     pl.when(early > 0)(lambda: pl.semaphore_wait(barrier, early))
     pl.when(has_before)(lambda: reply(0, before))
 
-    slots = row_slots(chips)
 
     def send(src, dst, recv_sem, device):
         pltpu.make_async_remote_copy(
@@ -191,8 +187,11 @@
         def _():
             arrived(gathered.at[1, turned(side)], spare_recv.at[side])
 
-    def col_event(step, chunk, lane=None):
-        mine = (core >= 0) if lane is None else (core == lane)
+    def lanes(lane):
+        return (core >= 0) if lane is None else (core == lane)
+
+    def col_wait(step, chunk, lane=None):
+        mine = lanes(lane)
         for way in range(2):
             cut = way == 1 and step == 1 and chunk == 0
             for short in range(1 + cut):
@@ -201,10 +200,16 @@
                     owner = col - step if way == 0 else col + step
                     arrived(col_slot(owner, chunk, short), col_recv.at[owner - way, chunk])
 
-            if step < n_col - 1:
-                @pl.when(mine & sends(way, step + 1))
+    def col_pass(step, chunk, lane=None):
+        if step < n_col - 1:
+            for way in range(2):
+                @pl.when(lanes(lane) & sends(way, step + 1))
                 def _():
                     col_copy(way, step + 1, chunk).start()
+
+    def col_event(step, chunk, lane=None):
+        col_wait(step, chunk, lane)
+        col_pass(step, chunk, lane)
 
     def drain():
         for count in range(1, n_col):
@@ -224,12 +229,12 @@
         offset = (1 - step) if way == 0 else (step - 1)
         send(
             src, strip(offset, core, chunk),
-            row_recv.at[slots[way, step, chunk]],
+            row_recv.at[step - 1],
             row_next if way == 0 else row_prev,
         )
 
     def share_strip(offset, chunk, src):
-        send(src, strip(offset, core, chunk), sib_recv.at[chunk], sibling)
+        send(src, strip(offset, core, chunk), sib_recv, sibling)
 
     def row_own(chunk):
         src = row_block.at[:, pl.ds(chunk * wide, wide)]
@@ -237,23 +242,19 @@
             if reach(chips, chunk)[way] >= 1:
                 row_send_to(way, 1, chunk, src)
 
-    def row_event(step, chunk):
-        for way in range(2):
-            limit = reach(chips, chunk)[way]
-            if step <= limit:
-                offset = -step if way == 0 else step
-                slot = strip(offset, core, chunk)
-                arrived(slot, row_recv.at[slots[way, step, chunk]])
-                if step < limit:
-                    row_send_to(way, step + 1, chunk, slot)
-                share_strip(offset, chunk, slot)
-
-    def row_shared(chunk):
-        block = strips.at[pl.ds(0, chips * depth), pl.ds(chunk * wide, wide)]
-        arrived(block, sib_recv.at[chunk])
+    def row_event(step):
+        due = strips_due(chips, step) * wide // cols
+        arrived(strips.at[pl.ds(0, due * depth)], row_recv.at[step - 1])
+        for chunk in range(ROW_CHUNKS):
+            for way, limit in enumerate(reach(chips, chunk)):
+                if step <= limit:
+                    offset = -step if way == 0 else step
+                    slot = strip(offset, core, chunk)
+                    if step < limit:
+                        row_send_to(way, step + 1, chunk, slot)
+                    share_strip(offset, chunk, slot)
 
     def make_upper(chunk):
-        row_shared(chunk)
         at = pl.ds(chunk * wide, wide)
         for i in range(order // BLOCK):
             end = (i + 1) * BLOCK
@@ -316,24 +317,32 @@
 
     row_depth = max(max(reach(chips, r)) for r in range(ROW_CHUNKS))
     last = len(pieces) - 1
-    row_left = [(step, r) for step in range(1, row_depth + 1) for r in range(ROW_CHUNKS)]
     col_left = [(step, k) for step in range(2, n_col - 1) for k in range(len(pieces))]
-    col_event(1, 0, 0)
-    row_event(*row_left.pop(0))
-    col_event(1, 1)
+    for chunk in range(2):
+        col_event(1, chunk, 0)
+    col_wait(1, 1, 1)
+
+    @pl.when(held)
+    def _():
+        load_l.start()
+        load_l.wait()
+
     col_event(1, 0, 1)
+    col_pass(1, 1, 1)
     for chunk in range(2, len(pieces)):
         col_event(1, chunk)
-    while row_left and row_left[0][0] == 1:
-        row_event(*row_left.pop(0))
+    row_event(1)
     for side in range(2):
         turn_event(side)
-    while row_left:
-        row_event(*row_left.pop(0))
+    for step in range(2, row_depth + 1):
         if col_left:
             col_event(*col_left.pop(0))
+        row_event(step)
+    if col_left:
+        col_event(*col_left.pop(0))
+    arrived(strips.at[pl.ds(0, chips * depth)], sib_recv)
     mine_r.wait()
-    load_l.wait()
+    pl.when(free)(lambda: load_l.wait())
     load_u.wait()
     for chunk in range(ROW_CHUNKS):
         make_upper(chunk)
@@ -432,8 +441,8 @@
             dma((2,)),
             dma((n_col - 1, count)),
             dma,
-            dma((len(row_slots(chips)),)),
-            dma((ROW_CHUNKS,)),
+            dma((chips // 2,)),
+            dma,
             dma((2,)),
             dma((2,)),
             pltpu.SemaphoreType.REGULAR((4,)),

time: 31.5 us -> 31.5 us (level)
  no operation moved by 1% of the time
where the time goes in v4:
time: 31.5 us; the launch traced here: 31.2 us
  Pallas kernels  30.6 us (97%)
  between operations  0.64 us (2%)
    pallas_call x1, Pallas kernels, on_device(): pl.pallas_call(functools.partial(kernel, n_row, n_col), out_shape=(tile,...  28.7 us
    pallas_call x1, Pallas kernels, on_device(): pl.pallas_call(functools.partial(finish, n_col), out_shape=(tile, jax.Sha...  1.89 us

profile of v4, /device:TPU:0, one launch (start us, length us, event | category | flops | bytes accessed | tf_op | source)
XLA Modules:
  0.0 31.2 jit_solution(5835443519227104788)
XLA Ops:
  0.6 28.7 %shard_map.76 = (bf16[768,256]{1,0:T(8,128)(2,1)S(1)}, bf16[4,768,256]{2,1,0:T(8,128)(2,1)S(1)}, bf16[1024,1024]{1,0:T(8,128)(2,1)S(1)}, bf16[1024,1024]{1,0:T(8,128)(2,1)S(1)}, f32[768,1024]{1,0:T(8,128)S(1)}) custom-call(f32[768,1024]{1,0:T(8,128)} %trailing.1, bf16[768,256]{1,0:T(8,128)(2,1)} %column_block.1, bf16[128,1024]{1,0:T(8,128)(2,1)} %row_block.1, ...), custom_call_target="tpu_custom_call" | custom-call | tf_op jit(solution)/shard_map/pallas_call | solution.py:424
  29.3 1.9 %shard_map.77 = (bf16[768,256]{1,0:T(8,128)(2,1)}, bf16[128,1024]{1,0:T(8,128)(2,1)}, f32[768,1024]{1,0:T(8,128)}) custom-call(bf16[768,256]{1,0:T(8,128)(2,1)S(1)} %get-tuple-element.8.lower_done, bf16[4,768,256]{2,1,0:T(8,128)(2,1)S(1)} %get-tuple-element.9.gathered, bf16[1024,1024]{1,0:T(8,128)(2,1)S(1)} %get-tuple-element.10.uinv, ...), custom_call_target="tpu_custom_call" | custom-call | tf_op jit(solution)/shard_map/pallas_call | solution.py:454

commit v5 on v4

--- a/solution.py
+++ b/solution.py
@@ -11,7 +11,7 @@
 BLOCK = 256
 PARTS = (3, 3, 2)
 ROW_CHUNKS = 2
-DETOUR = 16
+DETOUR = 24
 
 
 def chunks_of(rows):
@@ -28,6 +28,11 @@
 
 def strips_due(chips, step):
     return sum(limit >= step for r in range(ROW_CHUNKS) for limit in reach(chips, r))
+
+
+def turn_stops(chips):
+    stops = [(1,), (chips - 1,), (1, 2)]
+    return stops if chips > 3 else stops[:2]
 
 
 def kernel(
@@ -44,36 +49,12 @@
     wide = cols // ROW_CHUNKS
     row, col = lax.axis_index("row"), lax.axis_index("col")
     chips = n_row // 2
-    half = chips // 2
     core = lax.rem(row, 2)
-
-    def snake(place):
-        return place + (place // half) * (chips + half - 1 - 2 * place)
-
-    place = snake(row // 2)
-
-    def chip_at(offset):
-        return snake(lax.rem(place + chips + offset, chips))
-
-    sibling = {"row": row + 1 - 2 * core}
-    next_row = chip_at(1) * 2 + core
-    prev_row = chip_at(-1) * 2 + core
-    row_next = {"row": next_row}
-    row_prev = {"row": prev_row}
-    next_later = next_row > row
-    prev_later = prev_row > row
     after = {"col": col + 1}
     before = {"col": col - 1}
     has_after = col < n_col - 1
     has_before = col > 0
 
-    load_l = pltpu.make_async_copy(lower_inv, linv, local_sem.at[0])
-    load_u = pltpu.make_async_copy(upper_inv, uinv, local_sem.at[1])
-    load_t = pltpu.make_async_copy(trailing, updated, local_sem.at[2])
-    mine_c = pltpu.make_async_copy(column_block, gathered.at[col], local_sem.at[3])
-    my_rows = pl.ds(pl.multiple_of(row * depth, depth), depth)
-    mine_r = pltpu.make_async_copy(row_block, strips.at[my_rows], local_sem.at[4])
-
     barrier = pltpu.get_barrier_semaphore()
 
     def greet(device):
@@ -91,34 +72,22 @@
         pl.semaphore_wait(met.at[index], 1)
 
     pl.when(has_after)(lambda: greet(after))
-    pl.when(even & next_later)(lambda: greet(row_next))
-    pl.when(even & prev_later)(lambda: greet(row_prev))
-    pl.when(even & (core == 0))(lambda: greet(sibling))
-    mine_c.start()
-    mine_r.start()
-    pl.when(free)(lambda: load_l.start())
-    load_u.start()
-    behind = (col + n_col - 1) // n_col
-    below = (row - next_row + n_row) // n_row + (row - prev_row + n_row) // n_row
-    early = behind + (core + below) * (1 - odd)
-    pl.when(early > 0)(lambda: pl.semaphore_wait(barrier, early))
-    pl.when(has_before)(lambda: reply(0, before))
-
-
-    def send(src, dst, recv_sem, device):
-        pltpu.make_async_remote_copy(
-            src_ref=src, dst_ref=dst, send_sem=row_send, recv_sem=recv_sem,
-            device_id=device, device_id_type=MESH,
-        ).start()
+
+    @pl.when(odd == 1)
+    def _():
+        pl.semaphore_wait(barrier, 1)
+        reply(0, before)
+
 
     def arrived(dst, sem):
         pltpu.make_async_copy(dst, dst, sem).wait()
 
     turn = rows // DETOUR
+    stops = turn_stops(chips)
 
     def span(chunk, short):
         start, size = pieces[chunk]
-        return pl.ds(start, size - 2 * turn if short else size)
+        return pl.ds(start, size - len(stops) * turn if short else size)
 
     def col_slot(owner, chunk, short=False):
         return gathered.at[owner, span(chunk, short)]
@@ -144,43 +113,94 @@
     def takes(way, step):
         return col >= step if way == 0 else col + step < n_col
 
-    def col_own(way):
-        for short in range(1 + way):
-            @pl.when(sends(way, 1) & turns(1, short) if way else sends(way, 1))
+    def col_own(way, where, bends=0):
+        for short in range(1 + bends):
+            @pl.when(sends(way, 1) & where & turns(1, short) if bends else sends(way, 1) & where)
             def _():
                 for chunk in range(len(pieces)):
                     col_copy(way, 1, chunk, short and chunk == 0).start()
 
     def turns(at, short):
-        here = (place == 0) & (col == at)
-        return here if short else (place != 0) | (col != at)
+        return (row < 2) & (col == at) if short else (row >= 2) | (col != at)
+
+    col_own(1, odd == 1, 1)
+    half = chips // 2
+
+    def snake(place):
+        return place + (place // half) * (chips + half - 1 - 2 * place)
+
+    place = snake(row // 2)
+
+    def chip_at(offset):
+        return snake(lax.rem(place + chips + offset, chips))
+
+    sibling = {"row": row + 1 - 2 * core}
+    next_row = chip_at(1) * 2 + core
+    prev_row = chip_at(-1) * 2 + core
+    row_next = {"row": next_row}
+    row_prev = {"row": prev_row}
+    next_later = next_row > row
+    prev_later = prev_row > row
+    load_l = pltpu.make_async_copy(lower_inv, linv, local_sem.at[0])
+    load_u = pltpu.make_async_copy(upper_inv, uinv, local_sem.at[1])
+    load_t = pltpu.make_async_copy(trailing, updated, local_sem.at[2])
+    mine_c = pltpu.make_async_copy(column_block, gathered.at[col], local_sem.at[3])
+    my_rows = pl.ds(pl.multiple_of(row * depth, depth), depth)
+    mine_r = pltpu.make_async_copy(row_block, strips.at[my_rows], local_sem.at[4])
+
+    pl.when(even & next_later)(lambda: greet(row_next))
+    pl.when(even & prev_later)(lambda: greet(row_prev))
+    pl.when(even & (core == 0))(lambda: greet(sibling))
+    mine_c.start()
+    mine_r.start()
+    pl.when(free)(lambda: load_l.start())
+    load_u.start()
+    below = (row - next_row + n_row) // n_row + (row - prev_row + n_row) // n_row
+    early = ((col + n_col - 1) // n_col + core + below) * (1 - odd)
+    pl.when(early > 0)(lambda: pl.semaphore_wait(barrier, early))
+    pl.when(even & has_before)(lambda: reply(0, before))
+    col_own(1, even)
+
+    def send(src, dst, recv_sem, device):
+        pltpu.make_async_remote_copy(
+            src_ref=src, dst_ref=dst, send_sem=row_send, recv_sem=recv_sem,
+            device_id=device, device_id_type=MESH,
+        ).start()
 
     def turned(side):
-        return pl.ds(pieces[0][1] - (2 - side) * turn, turn)
-
-    def turning(side):
-        return (place == (chips - 1 if side else 1)) & (col == 1)
+        return pl.ds(pieces[0][1] - (len(stops) - side) * turn, turn)
+
+    def turn_copy(side, src, dst, send_sem, device):
+        pltpu.make_async_remote_copy(
+            src_ref=src, dst_ref=dst, send_sem=send_sem, recv_sem=spare_recv.at[side],
+            device_id=device, device_id_type=MESH,
+        ).start()
 
     def turn_own():
         @pl.when(turns(1, True))
         def _():
-            for side in range(2):
-                pltpu.make_async_remote_copy(
-                    src_ref=column_block.at[turned(side)], dst_ref=spare.at[side],
-                    send_sem=col_send.at[1], recv_sem=spare_recv.at[side],
-                    device_id=row_prev if side else row_next, device_id_type=MESH,
-                ).start()
-
-    def turn_event(side):
-        @pl.when(turning(side))
+            for side in range(len(stops)):
+                turn_copy(
+                    side, column_block.at[turned(side)], spare.at[side], col_send.at[1],
+                    row_prev if side == 1 else row_next,
+                )
+
+    def turning(stop):
+        return (place == stop) & (col == 1)
+
+    def turn_event(side, hop):
+        stop = stops[side][hop]
+
+        @pl.when(turning(stop))
         def _():
             arrived(spare.at[side], spare_recv.at[side])
-            pltpu.make_async_remote_copy(
-                src_ref=spare.at[side], dst_ref=gathered.at[1, turned(side)],
-                send_sem=spare_send.at[side], recv_sem=spare_recv.at[side],
-                device_id={"row": next_row if side else prev_row, "col": col - 1},
-                device_id_type=MESH,
-            ).start()
+            if hop + 1 < len(stops[side]):
+                turn_copy(side, spare.at[side], spare.at[side], spare_send.at[side], row_next)
+            else:
+                turn_copy(
+                    side, spare.at[side], gathered.at[1, turned(side)], spare_send.at[side],
+                    {"row": chip_at(-stop) * 2 + core, "col": col - 1},
+                )
 
     def turn_last(side):
         @pl.when(turns(0, True))
@@ -217,8 +237,9 @@
             pl.when(col + 1 == count)(lambda: arrived(block, col_send.at[0]))
             pl.when(n_col - col == count)(lambda: arrived(block, col_send.at[1]))
         arrived(strips.at[pl.ds(0, (n_row - 1) * depth)], row_send)
-        for side in range(2):
-            pl.when(turning(side))(lambda: arrived(spare.at[side], spare_send.at[side]))
+        for side in range(len(stops)):
+            for stop in stops[side]:
+                pl.when(turning(stop))(lambda: arrived(spare.at[side], spare_send.at[side]))
 
     def strip(offset, lane, chunk):
         owner = chip_at(offset) * 2 + lane
@@ -287,13 +308,12 @@
         at = pl.ds(*pieces[chunk])
         updated[at] -= jnp.dot(lower[at], upper[...], preferred_element_type=jnp.float32)
 
-    col_own(1)
     pl.when(even & (prev_row < row))(lambda: reply(1, row_prev))
     pl.when(even & (next_row < row))(lambda: reply(1, row_next))
     pl.when(even & (core == 1))(lambda: reply(1, sibling))
     mine_c.wait()
     pl.when(has_after)(lambda: await_reply(0))
-    col_own(0)
+    col_own(0, has_after)
     late = (3 - core - below) * (1 - odd)
     pl.when(late > 0)(lambda: pl.semaphore_wait(met.at[1], late))
 
@@ -332,8 +352,10 @@
     for chunk in range(2, len(pieces)):
         col_event(1, chunk)
     row_event(1)
-    for side in range(2):
-        turn_event(side)
+    for side in range(len(stops)):
+        turn_event(side, 0)
+    if len(stops) > 2:
+        turn_event(2, 1)
     for step in range(2, row_depth + 1):
         if col_left:
             col_event(*col_left.pop(0))
@@ -351,7 +373,7 @@
     for step, chunk in col_left:
         col_event(step, chunk)
     load_t.wait()
-    for side in range(2):
+    for side in range(len(stops)):
         turn_last(side)
     for chunk in range(len(pieces)):
         if chunk == last:
@@ -436,15 +458,15 @@
             pltpu.VMEM((order, cols), narrow),
             pltpu.VMEM((order, order), narrow),
             pltpu.VMEM((rows, order), narrow),
-            pltpu.VMEM((2, rows // DETOUR, share), narrow),
+            pltpu.VMEM((len(turn_stops(chips)), rows // DETOUR, share), narrow),
             dma((5,)),
             dma((2,)),
             dma((n_col - 1, count)),
             dma,
             dma((chips // 2,)),
             dma,
-            dma((2,)),
-            dma((2,)),
+            dma((len(turn_stops(chips)),)),
+            dma((len(turn_stops(chips)),)),
             pltpu.SemaphoreType.REGULAR((4,)),
         ],
         compiler_params=pltpu.CompilerParams(

time: 31.5 us -> 31.3 us (level)
  no operation moved by 1% of the time
where the time goes in v5:
time: 31.3 us; the launch traced here: 31.2 us
  Pallas kernels  30.5 us (97%)
  between operations  0.64 us (2%)
    pallas_call x1, Pallas kernels, on_device(): pl.pallas_call(functools.partial(kernel, n_row, n_col), out_shape=(tile,...  28.6 us
    pallas_call x1, Pallas kernels, on_device(): pl.pallas_call(functools.partial(finish, n_col), out_shape=(tile, jax.Sha...  1.89 us

profile of v5, /device:TPU:0, one launch (start us, length us, event | category | flops | bytes accessed | tf_op | source)
XLA Modules:
  0.0 31.2 jit_solution(9699659920350903095)
XLA Ops:
  0.6 28.6 %shard_map.76 = (bf16[768,256]{1,0:T(8,128)(2,1)S(1)}, bf16[4,768,256]{2,1,0:T(8,128)(2,1)S(1)}, bf16[1024,1024]{1,0:T(8,128)(2,1)S(1)}, bf16[1024,1024]{1,0:T(8,128)(2,1)S(1)}, f32[768,1024]{1,0:T(8,128)S(1)}) custom-call(f32[768,1024]{1,0:T(8,128)} %trailing.1, bf16[768,256]{1,0:T(8,128)(2,1)} %column_block.1, bf16[128,1024]{1,0:T(8,128)(2,1)} %row_block.1, ...), custom_call_target="tpu_custom_call" | custom-call | tf_op jit(solution)/shard_map/pallas_call | solution.py:446
  29.3 1.9 %shard_map.77 = (bf16[768,256]{1,0:T(8,128)(2,1)}, bf16[128,1024]{1,0:T(8,128)(2,1)}, f32[768,1024]{1,0:T(8,128)}) custom-call(bf16[768,256]{1,0:T(8,128)(2,1)S(1)} %get-tuple-element.8.lower_done, bf16[4,768,256]{2,1,0:T(8,128)(2,1)S(1)} %get-tuple-element.9.gathered, bf16[1024,1024]{1,0:T(8,128)(2,1)S(1)} %get-tuple-element.10.uinv, ...), custom_call_target="tpu_custom_call" | custom-call | tf_op jit(solution)/shard_map/pallas_call | solution.py:476

commit v6 on v5

--- a/solution.py
+++ b/solution.py
@@ -31,8 +31,15 @@
 
 
 def turn_stops(chips):
-    stops = [(1,), (chips - 1,), (1, 2)]
-    return stops if chips > 3 else stops[:2]
+    return [(1,), (1, 2), (chips - 1,)] if chips > 3 else [(1,), (chips - 1,)]
+
+
+def turn_groups(chips):
+    groups = {}
+    for side, stops in enumerate(turn_stops(chips)):
+        for hop, stop in enumerate(stops):
+            groups.setdefault((hop, stop), []).append(side)
+    return [(hop, stop, sides) for (hop, stop), sides in sorted(groups.items())]
 
 
 def kernel(
@@ -114,7 +121,7 @@
         return col >= step if way == 0 else col + step < n_col
 
     def col_own(way, where, bends=0):
-        for short in range(1 + bends):
+        for short in reversed(range(1 + bends)):
             @pl.when(sends(way, 1) & where & turns(1, short) if bends else sends(way, 1) & where)
             def _():
                 for chunk in range(len(pieces)):
@@ -170,9 +177,9 @@
     def turned(side):
         return pl.ds(pieces[0][1] - (len(stops) - side) * turn, turn)
 
-    def turn_copy(side, src, dst, send_sem, device):
+    def turn_copy(src, dst, send_sem, device):
         pltpu.make_async_remote_copy(
-            src_ref=src, dst_ref=dst, send_sem=send_sem, recv_sem=spare_recv.at[side],
+            src_ref=src, dst_ref=dst, send_sem=send_sem, recv_sem=spare_recv,
             device_id=device, device_id_type=MESH,
         ).start()
 
@@ -181,31 +188,34 @@
         def _():
             for side in range(len(stops)):
                 turn_copy(
-                    side, column_block.at[turned(side)], spare.at[side], col_send.at[1],
-                    row_prev if side == 1 else row_next,
+                    column_block.at[turned(side)], spare.at[side], col_send.at[1],
+                    row_next if stops[side][0] == 1 else row_prev,
                 )
 
     def turning(stop):
         return (place == stop) & (col == 1)
 
-    def turn_event(side, hop):
-        stop = stops[side][hop]
-
+    def turn_block(sides):
+        return spare.at[pl.ds(sides[0], len(sides))]
+
+    def turn_event(hop, stop, sides):
         @pl.when(turning(stop))
         def _():
-            arrived(spare.at[side], spare_recv.at[side])
-            if hop + 1 < len(stops[side]):
-                turn_copy(side, spare.at[side], spare.at[side], spare_send.at[side], row_next)
-            else:
-                turn_copy(
-                    side, spare.at[side], gathered.at[1, turned(side)], spare_send.at[side],
-                    {"row": chip_at(-stop) * 2 + core, "col": col - 1},
-                )
-
-    def turn_last(side):
+            arrived(turn_block(sides), spare_recv)
+            for side in sides:
+                if hop + 1 < len(stops[side]):
+                    turn_copy(spare.at[side], spare.at[side], spare_send, row_next)
+                else:
+                    turn_copy(
+                        spare.at[side], gathered.at[1, turned(side)], spare_send,
+                        {"row": chip_at(-stop) * 2 + core, "col": col - 1},
+                    )
+
+    def turn_last():
         @pl.when(turns(0, True))
         def _():
-            arrived(gathered.at[1, turned(side)], spare_recv.at[side])
+            size = len(stops) * turn
+            arrived(gathered.at[1, pl.ds(pieces[0][1] - size, size)], spare_recv)
 
     def lanes(lane):
         return (core >= 0) if lane is None else (core == lane)
@@ -237,9 +247,8 @@
             pl.when(col + 1 == count)(lambda: arrived(block, col_send.at[0]))
             pl.when(n_col - col == count)(lambda: arrived(block, col_send.at[1]))
         arrived(strips.at[pl.ds(0, (n_row - 1) * depth)], row_send)
-        for side in range(len(stops)):
-            for stop in stops[side]:
-                pl.when(turning(stop))(lambda: arrived(spare.at[side], spare_send.at[side]))
+        for hop, stop, sides in turn_groups(chips):
+            pl.when(turning(stop))(lambda: arrived(turn_block(sides), spare_send))
 
     def strip(offset, lane, chunk):
         owner = chip_at(offset) * 2 + lane
@@ -322,7 +331,7 @@
         for device in (row_next, row_prev, sibling):
             reply(2, device)
 
-    pl.when(odd == 1)(lambda: await_reply(3))
+    pl.when(odd == 1)(lambda: await_reply(1))
     turn_own()
     for chunk in range(ROW_CHUNKS):
         row_own(chunk)
@@ -333,7 +342,7 @@
     @pl.when(even & has_after)
     def _():
         pl.semaphore_wait(met.at[2], 3)
-        reply(3, after)
+        reply(1, after)
 
     row_depth = max(max(reach(chips, r)) for r in range(ROW_CHUNKS))
     last = len(pieces) - 1
@@ -352,10 +361,8 @@
     for chunk in range(2, len(pieces)):
         col_event(1, chunk)
     row_event(1)
-    for side in range(len(stops)):
-        turn_event(side, 0)
-    if len(stops) > 2:
-        turn_event(2, 1)
+    for group in turn_groups(chips):
+        turn_event(*group)
     for step in range(2, row_depth + 1):
         if col_left:
             col_event(*col_left.pop(0))
@@ -373,8 +380,7 @@
     for step, chunk in col_left:
         col_event(step, chunk)
     load_t.wait()
-    for side in range(len(stops)):
-        turn_last(side)
+    turn_last()
     for chunk in range(len(pieces)):
         if chunk == last:
             drain()
@@ -465,9 +471,9 @@
             dma,
             dma((chips // 2,)),
             dma,
-            dma((len(turn_stops(chips)),)),
-            dma((len(turn_stops(chips)),)),
-            pltpu.SemaphoreType.REGULAR((4,)),
+            dma,
+            dma,
+            pltpu.SemaphoreType.REGULAR((3,)),
         ],
         compiler_params=pltpu.CompilerParams(
             collective_id=0, has_side_effects=True, vmem_limit_bytes=32 << 20

time: 31.3 us -> 31.3 us (level)
  no operation moved by 1% of the time
where the time goes in v6:
time: 31.3 us; the launch traced here: 31.1 us
  Pallas kernels  30.5 us (97%)
  between operations  0.64 us (2%)
    pallas_call x1, Pallas kernels, on_device(): pl.pallas_call(functools.partial(kernel, n_row, n_col), out_shape=(tile,...  28.6 us
    pallas_call x1, Pallas kernels, on_device(): pl.pallas_call(functools.partial(finish, n_col), out_shape=(tile, jax.Sha...  1.89 us

profile of v6, /device:TPU:0, one launch (start us, length us, event | category | flops | bytes accessed | tf_op | source)
XLA Modules:
  0.0 31.1 jit_solution(11660334084378975953)
XLA Ops:
  0.6 28.6 %shard_map.76 = (bf16[768,256]{1,0:T(8,128)(2,1)S(1)}, bf16[4,768,256]{2,1,0:T(8,128)(2,1)S(1)}, bf16[1024,1024]{1,0:T(8,128)(2,1)S(1)}, bf16[1024,1024]{1,0:T(8,128)(2,1)S(1)}, f32[768,1024]{1,0:T(8,128)S(1)}) custom-call(f32[768,1024]{1,0:T(8,128)} %trailing.1, bf16[768,256]{1,0:T(8,128)(2,1)} %column_block.1, bf16[128,1024]{1,0:T(8,128)(2,1)} %row_block.1, ...), custom_call_target="tpu_custom_call" | custom-call | tf_op jit(solution)/shard_map/pallas_call | solution.py:452
  29.2 1.9 %shard_map.77 = (bf16[768,256]{1,0:T(8,128)(2,1)}, bf16[128,1024]{1,0:T(8,128)(2,1)}, f32[768,1024]{1,0:T(8,128)}) custom-call(bf16[768,256]{1,0:T(8,128)(2,1)S(1)} %get-tuple-element.8.lower_done, bf16[4,768,256]{2,1,0:T(8,128)(2,1)S(1)} %get-tuple-element.9.gathered, bf16[1024,1024]{1,0:T(8,128)(2,1)S(1)} %get-tuple-element.10.uinv, ...), custom_call_target="tpu_custom_call" | custom-call | tf_op jit(solution)/shard_map/pallas_call | solution.py:482

commit v7 on v6

--- a/solution.py
+++ b/solution.py
@@ -9,7 +9,7 @@
 
 MESH = pl.DeviceIdType.MESH
 BLOCK = 256
-PARTS = (3, 3, 2)
+PARTS = (5, 4, 3)
 ROW_CHUNKS = 2
 DETOUR = 24
 

time: 31.3 us -> 31.2 us (level)
  no operation moved by 1% of the time
where the time goes in v7:
time: 31.2 us; the launch traced here: 30.8 us
  Pallas kernels  30.2 us (97%)
  between operations  0.64 us (2%)
    pallas_call x1, Pallas kernels, on_device(): pl.pallas_call(functools.partial(kernel, n_row, n_col), out_shape=(tile,...  28.3 us
    pallas_call x1, Pallas kernels, on_device(): pl.pallas_call(functools.partial(finish, n_col), out_shape=(tile, jax.Sha...  1.89 us

profile of v7, /device:TPU:0, one launch (start us, length us, event | category | flops | bytes accessed | tf_op | source)
XLA Modules:
  0.0 30.8 jit_solution(6855347322112528744)
XLA Ops:
  0.6 28.3 %shard_map.76 = (bf16[768,256]{1,0:T(8,128)(2,1)S(1)}, bf16[4,768,256]{2,1,0:T(8,128)(2,1)S(1)}, bf16[1024,1024]{1,0:T(8,128)(2,1)S(1)}, bf16[1024,1024]{1,0:T(8,128)(2,1)S(1)}, f32[768,1024]{1,0:T(8,128)S(1)}) custom-call(f32[768,1024]{1,0:T(8,128)} %trailing.1, bf16[768,256]{1,0:T(8,128)(2,1)} %column_block.1, bf16[128,1024]{1,0:T(8,128)(2,1)} %row_block.1, ...), custom_call_target="tpu_custom_call" | custom-call | tf_op jit(solution)/shard_map/pallas_call | solution.py:452
  28.9 1.9 %shard_map.77 = (bf16[768,256]{1,0:T(8,128)(2,1)}, bf16[128,1024]{1,0:T(8,128)(2,1)}, f32[768,1024]{1,0:T(8,128)}) custom-call(bf16[768,256]{1,0:T(8,128)(2,1)S(1)} %get-tuple-element.8.lower_done, bf16[4,768,256]{2,1,0:T(8,128)(2,1)S(1)} %get-tuple-element.9.gathered, bf16[1024,1024]{1,0:T(8,128)(2,1)S(1)} %get-tuple-element.10.uinv, ...), custom_call_target="tpu_custom_call" | custom-call | tf_op jit(solution)/shard_map/pallas_call | solution.py:482

commit v8 on v7

--- a/solution.py
+++ b/solution.py
@@ -160,8 +160,6 @@
     pl.when(even & (core == 0))(lambda: greet(sibling))
     mine_c.start()
     mine_r.start()
-    pl.when(free)(lambda: load_l.start())
-    load_u.start()
     below = (row - next_row + n_row) // n_row + (row - prev_row + n_row) // n_row
     early = ((col + n_col - 1) // n_col + core + below) * (1 - odd)
     pl.when(early > 0)(lambda: pl.semaphore_wait(barrier, early))
@@ -335,6 +333,8 @@
     turn_own()
     for chunk in range(ROW_CHUNKS):
         row_own(chunk)
+    pl.when(free)(lambda: load_l.start())
+    load_u.start()
     load_t.start()
     for chunk in range(ROW_CHUNKS):
         share_strip(0, chunk, row_block.at[:, pl.ds(chunk * wide, wide)])

time: 31.2 us -> 31.2 us (level)
  no operation moved by 1% of the time
where the time goes in v8:
time: 31.2 us; the launch traced here: 30.8 us
  Pallas kernels  30.2 us (97%)
  between operations  0.64 us (2%)
    pallas_call x1, Pallas kernels, on_device(): pl.pallas_call(functools.partial(kernel, n_row, n_col), out_shape=(tile,...  28.3 us
    pallas_call x1, Pallas kernels, on_device(): pl.pallas_call(functools.partial(finish, n_col), out_shape=(tile, jax.Sha...  1.89 us

profile of v8, /device:TPU:0, one launch (start us, length us, event | category | flops | bytes accessed | tf_op | source)
XLA Modules:
  0.0 30.8 jit_solution(7238168449136774362)
XLA Ops:
  0.6 28.3 %shard_map.76 = (bf16[768,256]{1,0:T(8,128)(2,1)S(1)}, bf16[4,768,256]{2,1,0:T(8,128)(2,1)S(1)}, bf16[1024,1024]{1,0:T(8,128)(2,1)S(1)}, bf16[1024,1024]{1,0:T(8,128)(2,1)S(1)}, f32[768,1024]{1,0:T(8,128)S(1)}) custom-call(f32[768,1024]{1,0:T(8,128)} %trailing.1, bf16[768,256]{1,0:T(8,128)(2,1)} %column_block.1, bf16[128,1024]{1,0:T(8,128)(2,1)} %row_block.1, ...), custom_call_target="tpu_custom_call" | custom-call | tf_op jit(solution)/shard_map/pallas_call | solution.py:452
  28.9 1.9 %shard_map.77 = (bf16[768,256]{1,0:T(8,128)(2,1)}, bf16[128,1024]{1,0:T(8,128)(2,1)}, f32[768,1024]{1,0:T(8,128)}) custom-call(bf16[768,256]{1,0:T(8,128)(2,1)S(1)} %get-tuple-element.8.lower_done, bf16[4,768,256]{2,1,0:T(8,128)(2,1)S(1)} %get-tuple-element.9.gathered, bf16[1024,1024]{1,0:T(8,128)(2,1)S(1)} %get-tuple-element.10.uinv, ...), custom_call_target="tpu_custom_call" | custom-call | tf_op jit(solution)/shard_map/pallas_call | solution.py:482
